TPU v7x, 256 devices: a whole 4x4x8 slice. The times are simulated.
256 devices in a mesh: tm: 32 (over z, y_hi, core), space: 8 (over y_lo, x).
Axes of the slice: x: 4, y: 4 (y_hi: 2, y_lo: 2; y = y_hi * 2 + y_lo), z: 8, core: 2. Of those that a mesh axis runs over, the one named last changes fastest.
Arguments:
- model: float32 [32, 8192, 1024], P('tm', 'space'), may hold values from -6 to 6
- kernels: float32 [3, 600, 8192], P(None, None, ('space', 'tm')), may hold values from -0.0390625 to 0.0390625
Outputs:
- data: float32 [32, 600, 1024], P('tm', None, 'space')
All inputs are finite; a program needn't handle non-finite values.
Results may differ from a plain program's by a relative error of at most 0.0003.
Values sent between devices are 32-bit elements; how exact they have to be, the bound alone decides.
A program may use at most 64 MiB of HBM per device.

v0:
```python
import jax
import jax.numpy as jnp
from jax import lax
from jax.sharding import PartitionSpec as P


def passed_along(block, axis, distance):
    devices = range(lax.axis_size(axis))
    route = [(i - distance, i) for i in devices if i - distance in devices]
    return lax.ppermute(block, axis, route)


def on_device(model, kernels):
    local_model = model[0]
    lag_count = kernels.shape[0]
    products = jnp.einsum(
        "lsp,pc->lsc",
        lax.all_gather(kernels, "tm", axis=2, tiled=True),
        local_model,
        precision=lax.Precision.HIGHEST,
        preferred_element_type=jnp.float32,
    )
    running = products[lag_count - 1]
    for lag_index in range(lag_count - 2, -1, -1):
        running = passed_along(running, "tm", 1) + products[lag_index]
    result = lax.psum_scatter(running, "space", scatter_dimension=1, tiled=True)
    return result[None]


def solution(mesh):
    return jax.shard_map(
        on_device,
        mesh=mesh,
        in_specs=(P("tm", "space", None), P(None, None, ("space", "tm"))),
        out_specs=P("tm", None, "space"),
        check_vma=False,
    )
```

profile of v0, /device:TPU:32, one launch (start us, length us, event | category | flops | bytes accessed | tf_op | source)
XLA Modules:
  0.0 261.7 jit_solution(11356863142729187960)
XLA Ops:
  6.5 0.0 all-gather.2.cloned.1.call-start
  6.5 0.7 all-gather.2.cloned.1.call-update
  7.3 0.0 reduce-scatter.2.cloned.1.call-start
  7.3 104.9 %all-gather.2.cloned.1.call-done = f32[3,600,1024]{1,2,0:T(8,128)} async-done(((f32[3,600,32]{1,2,0:T(8,128)}), f32[3,600,1024]{1,2,0:T(8,128)}) %all-gather.2.cloned.1.call-update) | async-done | bytes 7372816 | tf_op jit(solution)/shard_map/all_gather | solution.py:18
  112.2 27.5 %fusion = f32[3,600,1024]{2,1,0:T(8,128)S(1)} fusion(f32[3,600,1024]{1,2,0:T(8,128)} %all-gather.2.cloned.1.call-done, f32[1,1024,1024]{2,1,0:T(8,128)} %param.2), kind=kOutput, calls=%fused_computation | convolution fusion | flops 22649241600 | bytes 18939904 | tf_op jit(solution)/shard_map/lsp,pc->lsc/dot_general | solution.py:16
  139.7 0.2 slice_bitcast_fusion.2
  139.9 2.2 collective-permute-start
  142.1 31.5 %collective-permute-done = f32[600,1024]{1,0:T(8,128)S(1)} collective-permute-done((f32[600,1024]{1,0:T(8,128)S(1)}, f32[600,1024]{1,0:T(8,128)S(1)}, u32[]{:S(2)}, u32[]{:S(2)}) %collective-permute-start) | collective-permute-done | bytes 2457632 | tf_op jit(solution)/shard_map/ppermute | solution.py:10
  173.5 0.5 fusion.3
  174.0 1.9 collective-permute-start.1
  175.9 31.7 %collective-permute-done.1 = f32[600,1024]{1,0:T(8,128)S(1)} collective-permute-done((f32[600,1024]{1,0:T(8,128)S(1)}, f32[600,1024]{1,0:T(8,128)S(1)}, u32[]{:S(2)}, u32[]{:S(2)}) %collective-permute-start.1) | collective-permute-done | bytes 2457632 | tf_op jit(solution)/shard_map/ppermute | solution.py:10
  207.6 1.9 fusion.2
  209.5 0.0 reduce-scatter.2.cloned.1.call-update
  209.6 45.3 %reduce-scatter.2.cloned.1.call-done = f32[600,128]{1,0:T(8,128)} async-done(((f32[600,1024]{1,0:T(8,128)}), f32[600,128]{1,0:T(8,128)}) %reduce-scatter.2.cloned.1.call-update) | async-done | bytes 307216 | tf_op jit(solution)/shard_map/reduce_scatter | solution.py:26
Async XLA Ops:
  6.5 105.7 %all-gather.2.cloned.1.call-start = ((), (), s32[]{:S(2)}) async-start(), calls=%async_computation.1 | async-start | bytes 8110080 | tf_op jit(solution)/shard_map/all_gather | solution.py:18
  7.3 247.6 %reduce-scatter.2.cloned.1.call-start = ((), (), s32[]{:S(2)}) async-start(), calls=%async_computation.2 | async-start | bytes 2764800 | tf_op jit(solution)/shard_map/reduce_scatter | solution.py:26
  139.9 33.6 %collective-permute-start = (f32[600,1024]{1,0:T(8,128)S(1)}, f32[600,1024]{1,0:T(8,128)S(1)}, u32[]{:S(2)}, u32[]{:S(2)}) collective-permute-start(f32[600,1024]{1,0:T(8,128)S(1)} %slice_bitcast_fusion.2), channel_id=1, source_target_pairs={{0,8},{8,16},{16,24},{24,32},{32,40},{40,48},{48,56},{56,64},{64,7... | collective-permute-start | bytes 7372808 | tf_op jit(solution)/shard_map/ppermute | solution.py:10
  174.0 33.6 %collective-permute-start.1 = (f32[600,1024]{1,0:T(8,128)S(1)}, f32[600,1024]{1,0:T(8,128)S(1)}, u32[]{:S(2)}, u32[]{:S(2)}) collective-permute-start(f32[600,1024]{1,0:T(8,128)S(1)} %fusion.3), channel_id=1, source_target_pairs={{0,8},{8,16},{16,24},{24,32},{32,40},{40,48},{48,56},{56,64},{64,7... | collective-permute-start | bytes 7372808 | tf_op jit(solution)/shard_map/ppermute | solution.py:10
Sparse Core Ops, SparseCore 0:
  10.1 102.0 all-gather.1
  209.7 45.1 reduce-scatter.1
where the time goes:
time: 262 us
  waiting for transfers between devices  214 us (82%)
  matrix products  27.5 us (10%)
  between operations  13.4 us (5%)
  starting transfers between devices  4.12 us (2%)
    all_gather x1, waiting for transfers between devices, on_device(): lax.all_gather(kernels, 'tm', axis=2, tiled=True)  105 us
    ppermute x2, waiting for transfers between devices, passed_along(): return lax.ppermute(block, axis, route)  63.1 us
    reduce_scatter x1, waiting for transfers between devices, on_device(): result = lax.psum_scatter(running, 'space', scatter_dimension=1, tiled=True)  45.3 us
    dot_general x1, matrix products, on_device(): jnp.einsum('lsp,pc->lsc', lax.all_gather(kernels, 'tm', axis=2, tiled=Tru...  27.5 us
  transfers between devices with their start and end apart: 4, of which 4 were waited for; matrix products, arithmetic and copies ran while one was open for 0% of the time, Pallas kernels for 0%

commit v1 on v0

--- a/solution.py
+++ b/solution.py
@@ -15,7 +15,9 @@
     lag_count = kernels.shape[0]
     products = jnp.einsum(
         "lsp,pc->lsc",
-        lax.all_gather(kernels, "tm", axis=2, tiled=True),
+        jnp.concatenate(
+            lax.all_to_all(jnp.stack([kernels] * lax.axis_size("tm")), "tm", 0, 0), axis=2
+        ),
         local_model,
         precision=lax.Precision.HIGHEST,
         preferred_element_type=jnp.float32,

time: 262 us -> 348 us (1.33)
  blocking collectives: 0 us -> 186 us
  waiting for transfers between devices: 214 us -> 108 us
  local copies, waits for them, and re-layouts: 0.17 us -> 4.25 us
    all_to_all x0 -> x1, blocking collectives: none -> 186 us  [on_device(): lax.all_to_all(jnp.stack([kernels] * lax.axis_size('tm')), 'tm', 0, 0)]
    all_gather x1 -> x0, waiting for transfers between devices: 105 us -> none  [on_device(): lax.all_gather(kernels, 'tm', axis=2, tiled=True)]
  transfers between devices with their start and end apart: 4 -> 3, of which waited for: 4 -> 3; matrix products, arithmetic and copies ran while one was open for 0% -> 0% of each run, Pallas kernels for 0% -> 0%
where the time goes in v1:
time: 348 us; the launch traced here: 347 us
  blocking collectives  186 us (53%)
  waiting for transfers between devices  108 us (31%)
  matrix products  29.4 us (8%)
  between operations  13.4 us (4%)
  local copies, waits for them, and re-layouts  4.25 us (1%)
  starting transfers between devices  3.84 us (1%)
    all_to_all x1, blocking collectives, on_device(): lax.all_to_all(jnp.stack([kernels] * lax.axis_size('tm')), 'tm', 0, 0)  186 us
    ppermute x2, waiting for transfers between devices, passed_along(): return lax.ppermute(block, axis, route)  63.4 us
    reduce_scatter x1, waiting for transfers between devices, on_device(): result = lax.psum_scatter(running, 'space', scatter_dimension=1, tiled=True)  44.7 us
    dot_general x1, matrix products, on_device(): jnp.einsum('lsp,pc->lsc', jnp.concatenate(lax.all_to_all(jnp.stack([kerne...  29.4 us
  transfers between devices with their start and end apart: 3, of which 3 were waited for; matrix products, arithmetic and copies ran while one was open for 0% of the time, Pallas kernels for 0%

profile of v1, /device:TPU:32, one launch (start us, length us, event | category | flops | bytes accessed | tf_op | source)
XLA Modules:
  0.0 347.4 jit_solution(11646270161508642864)
XLA Ops:
  6.5 0.0 reduce-scatter.2.cloned.1.call-start
  6.5 1.9 stack.2
  8.4 186.0 %all_to_all.5 = f32[32,3,600,32]{2,3,1,0:T(8,128)S(1)} all-to-all(f32[32,3,600,32]{2,3,1,0:T(8,128)S(1)} %stack.2), channel_id=1, replica_groups=mesh['tm'=32,'space'=8] {'tm'}, dimensions={0} | all-to-all | bytes 14745600 | tf_op jit(solution)/shard_map/all_to_all | solution.py:19
  194.4 0.0 copy-start
  194.4 0.7 copy.5
  195.1 1.5 copy-done
  196.6 29.4 %fusion = f32[3,600,1024]{2,1,0:T(8,128)S(1)} fusion(f32[3,600,1024]{1,2,0:T(8,128)S(1)} %bitcast.19, f32[1,1024,1024]{2,1,0:T(8,128)S(1)} %copy-done), kind=kOutput, calls=%fused_computation | convolution fusion | flops 22649241600 | bytes 18939904 | tf_op jit(solution)/shard_map/lsp,pc->lsc/dot_general | solution.py:16
  226.0 0.2 slice_bitcast_fusion.2
  226.2 1.9 collective-permute-start
  228.1 31.7 %collective-permute-done = f32[600,1024]{1,0:T(8,128)S(1)} collective-permute-done((f32[600,1024]{1,0:T(8,128)S(1)}, f32[600,1024]{1,0:T(8,128)S(1)}, u32[]{:S(2)}, u32[]{:S(2)}) %collective-permute-start) | collective-permute-done | bytes 2457632 | tf_op jit(solution)/shard_map/ppermute | solution.py:10
  259.8 0.5 fusion.3
  260.3 1.9 collective-permute-start.1
  262.2 31.7 %collective-permute-done.1 = f32[600,1024]{1,0:T(8,128)S(1)} collective-permute-done((f32[600,1024]{1,0:T(8,128)S(1)}, f32[600,1024]{1,0:T(8,128)S(1)}, u32[]{:S(2)}, u32[]{:S(2)}) %collective-permute-start.1) | collective-permute-done | bytes 2457632 | tf_op jit(solution)/shard_map/ppermute | solution.py:10
  293.9 1.9 fusion.2
  295.8 0.0 reduce-scatter.2.cloned.1.call-update
  295.8 44.7 %reduce-scatter.2.cloned.1.call-done = f32[600,128]{1,0:T(8,128)} async-done(((f32[600,1024]{1,0:T(8,128)}), f32[600,128]{1,0:T(8,128)}) %reduce-scatter.2.cloned.1.call-update) | async-done | bytes 307216 | tf_op jit(solution)/shard_map/reduce_scatter | solution.py:28
Async XLA Ops:
  6.5 334.0 %reduce-scatter.2.cloned.1.call-start = ((), (), s32[]{:S(2)}) async-start(), calls=%async_computation.2 | async-start | bytes 2764800 | tf_op jit(solution)/shard_map/reduce_scatter | solution.py:28
  194.4 2.2 copy-start
  226.2 33.6 %collective-permute-start = (f32[600,1024]{1,0:T(8,128)S(1)}, f32[600,1024]{1,0:T(8,128)S(1)}, u32[]{:S(2)}, u32[]{:S(2)}) collective-permute-start(f32[600,1024]{1,0:T(8,128)S(1)} %slice_bitcast_fusion.2), channel_id=1, source_target_pairs={{0,8},{8,16},{16,24},{24,32},{32,40},{40,48},{48,56},{56,64},{64,7... | collective-permute-start | bytes 7372808 | tf_op jit(solution)/shard_map/ppermute | solution.py:10
  260.3 33.6 %collective-permute-start.1 = (f32[600,1024]{1,0:T(8,128)S(1)}, f32[600,1024]{1,0:T(8,128)S(1)}, u32[]{:S(2)}, u32[]{:S(2)}) collective-permute-start(f32[600,1024]{1,0:T(8,128)S(1)} %fusion.3), channel_id=1, source_target_pairs={{0,8},{8,16},{16,24},{24,32},{32,40},{40,48},{48,56},{56,64},{64,7... | collective-permute-start | bytes 7372808 | tf_op jit(solution)/shard_map/ppermute | solution.py:10
Sparse Core Ops, SparseCore 0:
  296.0 44.5 reduce-scatter.1
